TPU v7x, 32 devices: a whole 2x2x4 slice. The times are simulated.
32 devices in a mesh: seq: 4 (over y, core), tp: 8 (over z, x).
Axes of the slice: x: 2, y: 2, z: 4, core: 2. Of those that a mesh axis runs over, the one named last changes fastest.
Arguments:
- tokens: bfloat16 [2048, 8192], P('seq', 'tp'), may hold values from -6 to 6
- w_query: bfloat16 [8192, 6144], P(None, 'tp'), may hold values from -0.0625 to 0.0625
- w_key: bfloat16 [8192, 6144], P(None, 'tp'), may hold values from -0.0625 to 0.0625
- w_value: bfloat16 [8192, 6144], P(None, 'tp'), may hold values from -0.0625 to 0.0625
- w_out: bfloat16 [6144, 8192], P('tp'), may hold values from -0.109375 to 0.109375
- carry: float32 [48, 128, 128], P('tp'), may hold values from -40 to 40
Outputs:
- mixed: bfloat16 [2048, 8192], P('seq', 'tp')
All inputs are finite; a program needn't handle non-finite values.
Results may differ from a plain program's by a relative error of at most 0.0066.
Values may be sent and summed in bfloat16 or wider, within the bound.
No kernel may reach another device: no remote copies, remote signals or barrier semaphores. Data moves between devices by JAX's collectives and lax.ppermute only.
A program may use at most 192 MiB of HBM per device.

v0:
```python
import jax
import jax.numpy as jnp
from jax import lax
from jax.sharding import PartitionSpec as P

EPSILON = 1e-05


def entering(array, axis, combine, identity):
    count, place = (lax.axis_size(axis), lax.axis_index(axis))
    everything = lax.all_gather(array, axis)
    start = jnp.broadcast_to(jnp.asarray(identity, array.dtype), array.shape)

    def turn(k, before):
        reached = k < place
        new = combine(before, everything[k])
        return jnp.where(reached, new, before)

    return lax.fori_loop(0, count, turn, start)


def combine_states(earlier, latter_part):
    return earlier + latter_part


def local(tokens, w_query, w_key, w_value, w_out, carry):
    row_count = tokens.shape[0]
    head_count = carry.shape[0]
    head_size = carry.shape[1]
    proj_width = w_query.shape[1]
    segment = lax.all_gather(tokens, "tp", axis=1, tiled=True)
    query_sum = jnp.dot(segment, w_query, preferred_element_type=jnp.float32)
    key_sum = jnp.dot(segment, w_key, preferred_element_type=jnp.float32)
    value_sum = jnp.dot(segment, w_value, preferred_element_type=jnp.float32)
    query = query_sum.astype(jnp.bfloat16).reshape(row_count, head_count, head_size)
    keys_local = key_sum.astype(jnp.bfloat16).reshape(row_count, head_count, head_size)
    values_local = value_sum.astype(jnp.bfloat16).reshape(row_count, head_count, head_size)
    local_state = jnp.einsum(
        "thd,the->hde", keys_local, values_local, preferred_element_type=jnp.float32
    )
    earlier_sum = entering(local_state, "seq", combine_states, jnp.zeros_like(local_state))
    prior = carry + earlier_sum
    across = jnp.einsum(
        "thd,hde->the", query.astype(jnp.float32), prior, precision=lax.Precision.HIGHEST
    )
    causal = lax.broadcasted_iota(jnp.int32, (row_count, row_count), 0) >= lax.broadcasted_iota(
        jnp.int32, (row_count, row_count), 1
    )
    scores = jnp.einsum("thd,shd->hts", query, keys_local, preferred_element_type=jnp.float32)
    scores = jnp.where(causal[None], scores, 0.0).astype(jnp.bfloat16)
    within = jnp.einsum("hts,she->the", scores, values_local, preferred_element_type=jnp.float32)
    total = across + within
    normed = total * lax.rsqrt(jnp.mean(total * total, axis=-1, keepdims=True) + EPSILON)
    attended = normed.astype(jnp.bfloat16).reshape(row_count, proj_width)
    summed = lax.psum_scatter(
        lax.dot_general(
            w_out, attended, (((0,), (1,)), ((), ())), preferred_element_type=jnp.float32
        ),
        "tp",
        scatter_dimension=0,
        tiled=True,
    )
    return summed.T.astype(jnp.bfloat16)


def solution(mesh):
    placed = (
        P("seq", "tp"),
        P(None, "tp"),
        P(None, "tp"),
        P(None, "tp"),
        P("tp", None),
        P("tp", None, None),
    )
    return jax.shard_map(
        local, mesh=mesh, in_specs=placed, out_specs=P("seq", "tp"), check_vma=False
    )
```

profile of v0, /device:TPU:0, one launch (start us, length us, event | category | flops | bytes accessed | tf_op | source)
XLA Modules:
  0.0 496.5 jit_solution(3666014107982523729)
XLA Ops:
  6.5 0.7 all-gather.4.cloned.1.call-update
  7.3 0.0 all-gather.6.cloned.1.call-start
  7.3 129.9 %all-gather.4.cloned.1.call-done = bf16[512,8192]{1,0:T(8,128)(2,1)} async-done(((bf16[512,1024]{1,0:T(8,128)(2,1)}), bf16[512,8192]{1,0:T(8,128)(2,1)}) %all-gather.4.cloned.1.call-update) | async-done | bytes 8388624 | tf_op jit(solution)/shard_map/all_gather | solution.py:31
  137.2 12.7 %convolution_convert_fusion.2 = bf16[512,768]{1,0:T(8,128)(2,1)S(1)} fusion(bf16[512,8192]{1,0:T(8,128)(2,1)} %all-gather.4.cloned.1.call-done, bf16[8192,768]{1,0:T(8,128)(2,1)} %param.10), kind=kOutput, calls=%fused_computation.14 | convolution fusion | flops 6442844160 | bytes 21757952 | tf_op jit(solution)/shard_map/dot_general | solution.py:33
  149.9 0.3 copy.18
  150.2 12.7 %convolution_convert_fusion.1 = bf16[512,768]{1,0:T(8,128)(2,1)S(1)} fusion(bf16[512,8192]{1,0:T(8,128)(2,1)} %all-gather.4.cloned.1.call-done, bf16[8192,768]{1,0:T(8,128)(2,1)} %param.11), kind=kOutput, calls=%fused_computation.13 | convolution fusion | flops 6442844160 | bytes 21757952 | tf_op jit(solution)/shard_map/dot_general | solution.py:34
  162.9 0.3 copy.19
  163.2 1.1 fusion.9
  164.3 0.0 all-gather.6.cloned.1.call-update
  164.3 0.2 reduce-scatter.2.cloned.1.call-start
  164.6 0.8 iota_compare_fusion
  165.3 13.2 %convolution_convert_fusion = bf16[512,768]{1,0:T(8,128)(2,1)S(1)} fusion(bf16[512,8192]{1,0:T(8,128)(2,1)} %all-gather.4.cloned.1.call-done, bf16[8192,768]{1,0:T(8,128)(2,1)} %param.9), kind=kOutput, calls=%fused_computation.12 | convolution fusion | flops 6442844160 | bytes 21757952 | tf_op jit(solution)/shard_map/dot_general | solution.py:32
  178.6 0.3 copy.21
  178.9 4.2 fusion
  183.1 4.6 while.14
  183.1 1.1 add_select_fusion.2
  184.2 1.1 add_select_fusion.2
  185.4 1.1 add_select_fusion.2
  186.5 1.1 add_select_fusion.2
  187.7 2.4 fusion.5
  190.1 0.2 fusion.6
  190.3 14.8 %convolution_bitcast_fusion = f32[8192,512]{0,1:T(8,128)} fusion(bf16[512,768]{0,1:T(8,128)(2,1)S(1)} %bitcast.34, bf16[768,8192]{1,0:T(8,128)(2,1)} %param.12), kind=kOutput, calls=%fused_computation.1 | convolution fusion | flops 6442450944 | bytes 30146560 | tf_op jit(solution)/shard_map/dot_general | solution.py:56
  205.1 282.1 %reduce-scatter.2.cloned.1.call-done = f32[1024,512]{0,1:T(8,128)} async-done(((f32[8192,512]{0,1:T(8,128)}), f32[1024,512]{0,1:T(8,128)}) %reduce-scatter.2.cloned.1.call-update) | async-done | bytes 2097168 | tf_op jit(solution)/shard_map/reduce_scatter | solution.py:55
  487.2 2.7 convert_bitcast_fusion
  (7 shorter events, 0.0 us)
Async XLA Ops:
  6.5 130.7 %all-gather.4.cloned.1.call-start = ((), (), s32[]{:S(2)}) async-start(), calls=%async_computation.1 | async-start | bytes 9437184 | tf_op jit(solution)/shard_map/all_gather | solution.py:31
  7.3 175.8 %all-gather.6.cloned.1.call-start = ((), (), s32[]{:S(2)}) async-start(), calls=%async_computation.3 | async-start | bytes 1966080 | tf_op jit(solution)/shard_map/all_gather | solution.py:11
  164.3 322.9 %reduce-scatter.2.cloned.1.call-start = ((), (), s32[]{:S(2)}) async-start(), calls=%async_computation.2 | async-start | bytes 18874368 | tf_op jit(solution)/shard_map/reduce_scatter | solution.py:55
  178.9 8.8 %copy-start = (f32[6,128,128]{2,1,0:T(8,128)S(1)}, f32[6,128,128]{2,1,0:T(8,128)}, u32[]{:S(2)}) copy-start(f32[6,128,128]{2,1,0:T(8,128)} %param.13) | copy-start | bytes 1179652
Sparse Core Ops, SparseCore 0:
  9.5 127.5 all-gather.3
  164.4 17.8 all-gather.5
  205.2 281.9 reduce-scatter.1
where the time goes:
time: 497 us; the launch traced here: 496 us
  waiting for transfers between devices  413 us (83%)
  matrix products  61.1 us (12%)
  between operations  13.2 us (3%)
  other arithmetic  8.24 us (2%)
    reduce_scatter x1, waiting for transfers between devices, local(): lax.psum_scatter(lax.dot_general(w_out, attended, (((0,), (1,)), ((), ())...  282 us
    all_gather x1, waiting for transfers between devices, local(): segment = lax.all_gather(tokens, 'tp', axis=1, tiled=True)  130 us
    dot_general x1, matrix products, local(): lax.dot_general(w_out, attended, (((0,), (1,)), ((), ())), preferred_elem...  14.8 us
    dot_general x1, matrix products, local(): query_sum = jnp.dot(segment, w_query, preferred_element_type=jnp.float32)  13.2 us
    dot_general x1, matrix products, local(): key_sum = jnp.dot(segment, w_key, preferred_element_type=jnp.float32)  12.7 us
    dot_general x1, matrix products, local(): value_sum = jnp.dot(segment, w_value, preferred_element_type=jnp.float32)  12.7 us
  transfers between devices with their start and end apart: 3, of which 2 were waited for; matrix products, arithmetic and copies ran while one was open for 4% of the time, Pallas kernels for 0%

commit v1 on v0

--- a/solution.py
+++ b/solution.py
@@ -24,11 +24,29 @@
 
 
 def local(tokens, w_query, w_key, w_value, w_out, carry):
+
+    def apply_numbers(inner_x):
+        total_devices = lax.psum(1, "tp")
+        samples = []
+        for q in range(total_devices):
+            samples.append((q, (q + 1) % total_devices))
+
+        def convert_lines(plain):
+            if len(plain) == total_devices:
+                return plain
+            a_next = lax.ppermute(plain[0], "tp", samples)
+            return convert_lines([a_next, *plain])
+
+        formed = convert_lines([inner_x])
+        b_now = jnp.concatenate(formed, axis=1)
+        x_new = lax.axis_index("tp")
+        return jnp.roll(b_now, (x_new + 1) * inner_x.shape[1], axis=1)
+
     row_count = tokens.shape[0]
     head_count = carry.shape[0]
     head_size = carry.shape[1]
     proj_width = w_query.shape[1]
-    segment = lax.all_gather(tokens, "tp", axis=1, tiled=True)
+    segment = apply_numbers(tokens)
     query_sum = jnp.dot(segment, w_query, preferred_element_type=jnp.float32)
     key_sum = jnp.dot(segment, w_key, preferred_element_type=jnp.float32)
     value_sum = jnp.dot(segment, w_value, preferred_element_type=jnp.float32)

time: 497 us -> 560 us (1.13)
  waiting for transfers between devices: 413 us -> 456 us
  local copies, waits for them, and re-layouts: 0.84 us -> 20.7 us
    ppermute x0 -> x7, waiting for transfers between devices: none -> 175 us  [convert_lines(): a_next = lax.ppermute(plain[0], 'tp', samples)]
    all_gather x1 -> x0, waiting for transfers between devices: 130 us -> none  [local(): segment = lax.all_gather(tokens, 'tp', axis=1, tiled=True)]
    unnamed x2 -> x31, local copies, waits for them, and re-layouts: 0.01 us -> 19.8 us
  transfers between devices with their start and end apart: 3 -> 9, of which waited for: 2 -> 8; matrix products, arithmetic and copies ran while one was open for 4% -> 3% of each run, Pallas kernels for 0% -> 0%
where the time goes in v1:
time: 560 us
  waiting for transfers between devices  456 us (81%)
  matrix products  58.2 us (10%)
  local copies, waits for them, and re-layouts  20.7 us (4%)
  between operations  13.7 us (2%)
  other arithmetic  8.25 us (1%)
    reduce_scatter x1, waiting for transfers between devices, local(): lax.psum_scatter(lax.dot_general(w_out, attended, (((0,), (1,)), ((), ())...  280 us
    ppermute x7, waiting for transfers between devices, convert_lines(): a_next = lax.ppermute(plain[0], 'tp', samples)  175 us
    unnamed x31, local copies, waits for them, and re-layouts  19.8 us
    dot_general x1, matrix products, local(): lax.dot_general(w_out, attended, (((0,), (1,)), ((), ())), preferred_elem...  14.8 us
    dot_general x1, matrix products, local(): query_sum = jnp.dot(segment, w_query, preferred_element_type=jnp.float32)  13.3 us
    dot_general x1, matrix products, local(): value_sum = jnp.dot(segment, w_value, preferred_element_type=jnp.float32)  12.7 us
  transfers between devices with their start and end apart: 9, of which 8 were waited for; matrix products, arithmetic and copies ran while one was open for 3% of the time, Pallas kernels for 0%

profile of v1, /device:TPU:0, one launch (start us, length us, event | category | flops | bytes accessed | tf_op | source)
XLA Modules:
  0.0 559.8 jit_solution(17653001376896906398)
XLA Ops:
  6.5 2.9 collective-permute-start
  9.5 26.5 %collective-permute-done = bf16[512,1024]{1,0:T(8,128)(2,1)S(1)} collective-permute-done((bf16[512,1024]{1,0:T(8,128)(2,1)}, bf16[512,1024]{1,0:T(8,128)(2,1)S(1)}, u32[]{:S(2)}, u32[]{:S(2)}) %collective-permute-start) | collective-permute-done | bytes 1048608 | tf_op jit(solution)/shard_map/ppermute | solution.py:37
  36.0 27.0 %collective-permute-done.1 = bf16[512,1024]{1,0:T(8,128)(2,1)S(1)} collective-permute-done((bf16[512,1024]{1,0:T(8,128)(2,1)S(1)}, bf16[512,1024]{1,0:T(8,128)(2,1)S(1)}, u32[]{:S(2)}, u32[]{:S(2)}) %collective-permute-start.1) | collective-permute-done | bytes 1048608 | tf_op jit(solution)/shard_map/ppermute | solution.py:37
  63.0 26.1 %collective-permute-done.2 = bf16[512,1024]{1,0:T(8,128)(2,1)S(1)} collective-permute-done((bf16[512,1024]{1,0:T(8,128)(2,1)S(1)}, bf16[512,1024]{1,0:T(8,128)(2,1)S(1)}, u32[]{:S(2)}, u32[]{:S(2)}) %collective-permute-start.2) | collective-permute-done | bytes 1048608 | tf_op jit(solution)/shard_map/ppermute | solution.py:37
  90.1 25.2 %collective-permute-done.3 = bf16[512,1024]{1,0:T(8,128)(2,1)S(1)} collective-permute-done((bf16[512,1024]{1,0:T(8,128)(2,1)S(1)}, bf16[512,1024]{1,0:T(8,128)(2,1)S(1)}, u32[]{:S(2)}, u32[]{:S(2)}) %collective-permute-start.3) | collective-permute-done | bytes 1048608 | tf_op jit(solution)/shard_map/ppermute | solution.py:37
  116.3 24.3 %collective-permute-done.4 = bf16[512,1024]{1,0:T(8,128)(2,1)S(1)} collective-permute-done((bf16[512,1024]{1,0:T(8,128)(2,1)S(1)}, bf16[512,1024]{1,0:T(8,128)(2,1)S(1)}, u32[]{:S(2)}, u32[]{:S(2)}) %collective-permute-start.4) | collective-permute-done | bytes 1048608 | tf_op jit(solution)/shard_map/ppermute | solution.py:37
  141.6 23.5 %collective-permute-done.5 = bf16[512,1024]{1,0:T(8,128)(2,1)} collective-permute-done((bf16[512,1024]{1,0:T(8,128)(2,1)S(1)}, bf16[512,1024]{1,0:T(8,128)(2,1)}, u32[]{:S(2)}, u32[]{:S(2)}) %collective-permute-start.5) | collective-permute-done | bytes 1048608 | tf_op jit(solution)/shard_map/ppermute | solution.py:37
  165.0 22.7 %collective-permute-done.6 = bf16[512,1024]{1,0:T(8,128)(2,1)} collective-permute-done((bf16[512,1024]{1,0:T(8,128)(2,1)}, bf16[512,1024]{1,0:T(8,128)(2,1)}, u32[]{:S(2)}, u32[]{:S(2)}) %collective-permute-start.6) | collective-permute-done | bytes 1048608 | tf_op jit(solution)/shard_map/ppermute | solution.py:37
  189.1 1.3 constant_dynamic-update-slice_fusion.14
  190.4 1.3 constant_dynamic-update-slice_fusion.13
  191.7 1.3 constant_dynamic-update-slice_fusion.12
  193.0 1.3 constant_dynamic-update-slice_fusion.11
  194.6 1.3 constant_dynamic-update-slice_fusion.8
  195.9 1.3 constant_dynamic-update-slice_fusion.7
  199.1 5.7 %copy-done.7 = bf16[512,16384]{1,0:T(8,128)(2,1)} copy-done((bf16[512,16384]{1,0:T(8,128)(2,1)}, bf16[512,16384]{1,0:T(8,128)(2,1)S(1)}, u32[]{:S(2)}) %copy-start.7) | copy-done | bytes 16777240
  204.9 9.7 %fusion.13 = bf16[512,768]{1,0:T(8,128)(2,1)S(1)} fusion(bf16[8192,768]{1,0:T(8,128)(2,1)} %param.10, bf16[512,16384]{1,0:T(8,128)(2,1)S(1)} %constant_dynamic-update-slice_fusion, s32[]{:T(128)S(6)} %select_n.39), kind=kOutput, calls=%fused_computation.18 | convolution fusion | flops 6442844160 | bytes 21757956 | tf_op jit(solution)/shard_map/dot_general | solution.py:51
  214.9 12.7 %fusion.16 = bf16[512,768]{1,0:T(8,128)(2,1)S(1)} fusion(bf16[8192,768]{1,0:T(8,128)(2,1)} %param.11, bf16[512,16384]{1,0:T(8,128)(2,1)} %copy-done.7, s32[]{:T(128)S(6)} %select_n.39), kind=kOutput, calls=%fused_computation.19 | convolution fusion | flops 6442844160 | bytes 21757956 | tf_op jit(solution)/shard_map/dot_general | solution.py:52
  230.0 13.3 %fusion.19 = bf16[512,768]{1,0:T(8,128)(2,1)S(1)} fusion(bf16[8192,768]{1,0:T(8,128)(2,1)} %param.9, bf16[512,16384]{1,0:T(8,128)(2,1)} %copy-done.7, s32[]{:T(128)S(6)} %select_n.39), kind=kOutput, calls=%fused_computation.20 | convolution fusion | flops 6442844160 | bytes 21757956 | tf_op jit(solution)/shard_map/dot_general | solution.py:50
  243.6 4.1 fusion.6
  247.7 4.6 while.14
  252.3 2.5 fusion.11
  255.1 14.8 %convolution_bitcast_fusion = f32[8192,512]{0,1:T(8,128)} fusion(bf16[512,768]{0,1:T(8,128)(2,1)S(1)} %bitcast.31, bf16[768,8192]{1,0:T(8,128)(2,1)} %param.12), kind=kOutput, calls=%fused_computation.1 | convolution fusion | flops 6442450944 | bytes 30146560 | tf_op jit(solution)/shard_map/dot_general | solution.py:74
  269.9 280.3 %reduce-scatter.2.cloned.1.call-done = f32[1024,512]{0,1:T(8,128)} async-done(((f32[8192,512]{0,1:T(8,128)}), f32[1024,512]{0,1:T(8,128)}) %reduce-scatter.2.cloned.1.call-update) | async-done | bytes 2097168 | tf_op jit(solution)/shard_map/reduce_scatter | solution.py:73
  550.2 2.7 convert_bitcast_fusion
  (48 shorter events, 14.0 us)
Async XLA Ops:
  6.5 192.5 %copy-start = (bf16[512,1024]{1,0:T(8,128)(2,1)S(1)}, bf16[512,1024]{1,0:T(8,128)(2,1)}, u32[]{:S(2)}) copy-start(bf16[512,1024]{1,0:T(8,128)(2,1)} %param.8) | copy-start | bytes 3145732
  6.5 241.2 %all-gather.3.cloned.1.call-start = ((), (), s32[]{:S(2)}) async-start(), calls=%async_computation.2 | async-start | bytes 1966080 | tf_op jit(solution)/shard_map/all_gather | solution.py:11
  6.5 29.4 %collective-permute-start = (bf16[512,1024]{1,0:T(8,128)(2,1)}, bf16[512,1024]{1,0:T(8,128)(2,1)S(1)}, u32[]{:S(2)}, u32[]{:S(2)}) collective-permute-start(bf16[512,1024]{1,0:T(8,128)(2,1)} %param.8), channel_id=1, source_target_pairs={{0,1},{1,2},{2,3},{3,4},{4,5},{5,6},{6,7},{7,0},{8,9},{9,10},{10,1... | collective-permute-start | bytes 3145736 | tf_op jit(solution)/shard_map/ppermute | solution.py:37
  36.0 27.0 %collective-permute-start.1 = (bf16[512,1024]{1,0:T(8,128)(2,1)S(1)}, bf16[512,1024]{1,0:T(8,128)(2,1)S(1)}, u32[]{:S(2)}, u32[]{:S(2)}) collective-permute-start(bf16[512,1024]{1,0:T(8,128)(2,1)S(1)} %collective-permute-done), channel_id=1, source_target_pairs={{0,1},{1,2},{2,3},{3,4},{4,5},{5,6},{6,7},{7,0},{8,9},{9,10},{10,1... | collective-permute-start | bytes 3145736 | tf_op jit(solution)/shard_map/ppermute | solution.py:37
  63.0 26.1 %collective-permute-start.2 = (bf16[512,1024]{1,0:T(8,128)(2,1)S(1)}, bf16[512,1024]{1,0:T(8,128)(2,1)S(1)}, u32[]{:S(2)}, u32[]{:S(2)}) collective-permute-start(bf16[512,1024]{1,0:T(8,128)(2,1)S(1)} %collective-permute-done.1), channel_id=1, source_target_pairs={{0,1},{1,2},{2,3},{3,4},{4,5},{5,6},{6,7},{7,0},{8,9},{9,10},{10,1... | collective-permute-start | bytes 3145736 | tf_op jit(solution)/shard_map/ppermute | solution.py:37
  89.1 1.0 copy-start.1
  90.1 25.2 %collective-permute-start.3 = (bf16[512,1024]{1,0:T(8,128)(2,1)S(1)}, bf16[512,1024]{1,0:T(8,128)(2,1)S(1)}, u32[]{:S(2)}, u32[]{:S(2)}) collective-permute-start(bf16[512,1024]{1,0:T(8,128)(2,1)S(1)} %collective-permute-done.2), channel_id=1, source_target_pairs={{0,1},{1,2},{2,3},{3,4},{4,5},{5,6},{6,7},{7,0},{8,9},{9,10},{10,1... | collective-permute-start | bytes 3145736 | tf_op jit(solution)/shard_map/ppermute | solution.py:37
  115.3 1.0 copy-start.3
  116.3 24.3 %collective-permute-start.4 = (bf16[512,1024]{1,0:T(8,128)(2,1)S(1)}, bf16[512,1024]{1,0:T(8,128)(2,1)S(1)}, u32[]{:S(2)}, u32[]{:S(2)}) collective-permute-start(bf16[512,1024]{1,0:T(8,128)(2,1)S(1)} %collective-permute-done.3), channel_id=1, source_target_pairs={{0,1},{1,2},{2,3},{3,4},{4,5},{5,6},{6,7},{7,0},{8,9},{9,10},{10,1... | collective-permute-start | bytes 3145736 | tf_op jit(solution)/shard_map/ppermute | solution.py:37
  140.6 1.0 copy-start.5
  141.6 23.5 %collective-permute-start.5 = (bf16[512,1024]{1,0:T(8,128)(2,1)S(1)}, bf16[512,1024]{1,0:T(8,128)(2,1)}, u32[]{:S(2)}, u32[]{:S(2)}) collective-permute-start(bf16[512,1024]{1,0:T(8,128)(2,1)S(1)} %collective-permute-done.4), channel_id=1, source_target_pairs={{0,1},{1,2},{2,3},{3,4},{4,5},{5,6},{6,7},{7,0},{8,9},{9,10},{10,1... | collective-permute-start | bytes 3145736 | tf_op jit(solution)/shard_map/ppermute | solution.py:37
  165.0 22.8 %collective-permute-start.6 = (bf16[512,1024]{1,0:T(8,128)(2,1)}, bf16[512,1024]{1,0:T(8,128)(2,1)}, u32[]{:S(2)}, u32[]{:S(2)}) collective-permute-start(bf16[512,1024]{1,0:T(8,128)(2,1)} %collective-permute-done.5), channel_id=1, source_target_pairs={{0,1},{1,2},{2,3},{3,4},{4,5},{5,6},{6,7},{7,0},{8,9},{9,10},{10,1... | collective-permute-start | bytes 3145736 | tf_op jit(solution)/shard_map/ppermute | solution.py:37
  165.0 33.5 %copy-start.6 = (bf16[512,1024]{1,0:T(8,128)(2,1)S(1)}, bf16[512,1024]{1,0:T(8,128)(2,1)}, u32[]{:S(2)}) copy-start(bf16[512,1024]{1,0:T(8,128)(2,1)} %copy-done.5) | copy-start | bytes 3145732
  165.0 33.6 %copy-start.4 = (bf16[512,1024]{1,0:T(8,128)(2,1)S(1)}, bf16[512,1024]{1,0:T(8,128)(2,1)}, u32[]{:S(2)}) copy-start(bf16[512,1024]{1,0:T(8,128)(2,1)} %copy-done.3) | copy-start | bytes 3145732
  165.0 33.7 %copy-start.2 = (bf16[512,1024]{1,0:T(8,128)(2,1)S(1)}, bf16[512,1024]{1,0:T(8,128)(2,1)}, u32[]{:S(2)}) copy-start(bf16[512,1024]{1,0:T(8,128)(2,1)} %copy-done.1) | copy-start | bytes 3145732
  199.1 5.8 %copy-start.7 = (bf16[512,16384]{1,0:T(8,128)(2,1)}, bf16[512,16384]{1,0:T(8,128)(2,1)S(1)}, u32[]{:S(2)}) copy-start(bf16[512,16384]{1,0:T(8,128)(2,1)S(1)} %constant_dynamic-update-slice_fusion) | copy-start | bytes 50331652
  229.0 321.2 %reduce-scatter.2.cloned.1.call-start = ((), (), s32[]{:S(2)}) async-start(), calls=%async_computation.1 | async-start | bytes 18874368 | tf_op jit(solution)/shard_map/reduce_scatter | solution.py:73
Sparse Core Ops, SparseCore 0:
  229.1 16.0 all-gather.2
  270.0 280.1 reduce-scatter.1
